TPU v7x, 32 devices: a whole 2x2x4 slice. The times are simulated.
32 devices in a mesh: shard: 2 (over y), tensor: 4 (over x, core), section: 4 (over z).
Axes of the slice: x: 2, y: 2, z: 4, core: 2. Of those that a mesh axis runs over, the one named last changes fastest.
Arguments:
- grad_parts: float32 [2, 4, 4, 1152, 1024], P('shard', 'tensor', 'section'), may hold values from -1 to 1
- master: float32 [1152, 16, 1024], P(('tensor', 'section'), 'shard'), may hold values from -0.1875 to 0.1875
- owner_map: int32 [4, 4], replicated, may hold values from 0 to 1, as said below
- left_factor: float32 [16, 1152, 1152], P('shard', ('tensor', 'section')), may hold values from -1.2 to 11.2, as said below
- right_factor: float32 [16, 1024, 1024], P('shard', ('tensor', 'section')), may hold values from -1.2 to 11.2, as said below
- left_basis: float32 [16, 1152, 1152], P('shard', ('tensor', 'section')), may hold values from -0.1875 to 0.1875
- right_basis: float32 [16, 1024, 1024], P('shard', None, ('tensor', 'section')), may hold values from -0.1875 to 0.1875
- moment_one: float32 [16, 1152, 1024], P('shard', ('tensor', 'section')), may hold values from -3 to 3
- moment_two: float32 [16, 1152, 1024], P('shard', ('tensor', 'section')), may hold values from 0.01 to 0.5
Outputs:
- new_master: float32 [1152, 16, 1024], P(('tensor', 'section'), 'shard')
- update_dir: float32 [1152, 16, 1024], P(('tensor', 'section'), 'shard')
- new_left: float32 [16, 1152, 1152], P('shard', ('tensor', 'section'))
- new_right: float32 [16, 1024, 1024], P('shard', ('tensor', 'section'))
- new_moment_one: float32 [16, 1152, 1024], P('shard', ('tensor', 'section'))
- new_moment_two: float32 [16, 1152, 1024], P('shard', ('tensor', 'section'))
Inputs may be any that keep to these rules, and one draw needn't show every extreme that they name: `owner_map`: each shard index owns exactly 8 matrices. `left_factor`: symmetric in its last two dimensions. `right_factor`: symmetric in its last two dimensions.
All inputs are finite; a program needn't handle non-finite values.
Results may differ from a plain program's by a relative error of at most 0.0003.
Values sent between devices are 32-bit elements; how exact they have to be, the bound alone decides.
A program may use at most 448 MiB of HBM per device.

v0:
```python
import jax
import jax.numpy as jnp
from jax import lax
from jax.sharding import PartitionSpec as P

beta_one = 0.95
beta_two = 0.95
epsilon = 1e-08
learn_rate = 0.01
decay_weight = 0.1
step_count = 10


def slot_table(owner_map, shards):
    owners_flat = owner_map.reshape(-1)
    matrices = owners_flat.shape[0]
    per_owner = matrices // shards
    member = (owners_flat[:, None] == jnp.arange(shards, dtype=jnp.int32)[None, :]).astype(
        jnp.int32
    )
    before = jnp.cumsum(member, axis=0) - member
    rank_in = jnp.sum(before * member, axis=1)
    slot_of = owners_flat * per_owner + rank_in
    places = (slot_of[:, None] == jnp.arange(matrices, dtype=jnp.int32)[None, :]).astype(jnp.int32)
    source = jnp.sum(places * jnp.arange(matrices, dtype=jnp.int32)[:, None], axis=0)
    return (slot_of, source)


def local(
    grad_parts,
    master,
    owner_map,
    left_factor,
    right_factor,
    left_basis,
    right_basis,
    moment_one,
    moment_two,
):
    exact_mode = lax.Precision.HIGHEST
    shards = lax.axis_size("shard")
    members = lax.axis_size(("tensor", "section"))
    position = lax.axis_index(("tensor", "section"))
    slot_of, source = slot_table(owner_map, shards)
    height = left_basis.shape[2]
    width = right_basis.shape[1]
    row_block = height // members
    col_block = width // members
    local_part = grad_parts[0, 0, 0]
    row_piece = lax.psum_scatter(local_part, "shard", scatter_dimension=0, tiled=True)
    stacked = lax.all_gather(row_piece[None], ("tensor", "section"), axis=0, tiled=True)
    ordered = jnp.take(stacked, source, axis=0)
    full_grad = lax.all_to_all(ordered, "shard", split_axis=0, concat_axis=1, tiled=True)
    full_right = lax.all_gather(right_basis, ("tensor", "section"), axis=2, tiled=True)
    grad_band = lax.dynamic_slice_in_dim(full_grad, position * row_block, row_block, 1)
    grad_slab = lax.dynamic_slice_in_dim(full_grad, position * col_block, col_block, 2)
    new_left = beta_two * left_factor + (1.0 - beta_two) * jnp.einsum(
        "orn,ofn->orf", grad_band, full_grad, precision=exact_mode
    )
    new_right = beta_two * right_factor + (1.0 - beta_two) * jnp.einsum(
        "ofc,ofn->ocn", grad_slab, full_grad, precision=exact_mode
    )
    turned = jnp.einsum("orf,ofn->orn", left_basis, full_grad, precision=exact_mode)
    rotated = jnp.einsum("orn,onk->ork", turned, full_right, precision=exact_mode)
    new_moment_one = beta_one * moment_one + (1.0 - beta_one) * rotated
    new_moment_two = beta_two * moment_two + (1.0 - beta_two) * rotated * rotated
    first_fix = 1.0 - beta_one**step_count
    second_fix = 1.0 - beta_two**step_count
    scaled = new_moment_one / first_fix / (jnp.sqrt(new_moment_two / second_fix) + epsilon)
    pulled = jnp.einsum("orn,okn->ork", scaled, full_right, precision=exact_mode)
    update_dir = lax.psum_scatter(
        jnp.einsum("orf,ork->fok", left_basis, pulled, precision=exact_mode),
        ("tensor", "section"),
        scatter_dimension=0,
        tiled=True,
    )
    new_master = master - learn_rate * (update_dir + decay_weight * master)
    return (new_master, update_dir, new_left, new_right, new_moment_one, new_moment_two)


def solution(mesh):
    placed = (
        P("shard", "tensor", "section", None, None),
        P(("tensor", "section"), "shard", None),
        P(),
        P("shard", ("tensor", "section"), None),
        P("shard", ("tensor", "section"), None),
        P("shard", ("tensor", "section"), None),
        P("shard", None, ("tensor", "section")),
        P("shard", ("tensor", "section"), None),
        P("shard", ("tensor", "section"), None),
    )
    return jax.shard_map(
        local,
        mesh=mesh,
        in_specs=placed,
        out_specs=(
            P(("tensor", "section"), "shard", None),
            P(("tensor", "section"), "shard", None),
            P("shard", ("tensor", "section"), None),
            P("shard", ("tensor", "section"), None),
            P("shard", ("tensor", "section"), None),
            P("shard", ("tensor", "section"), None),
        ),
        check_vma=False,
    )
```

profile of v0, /device:TPU:0, one launch (start us, length us, event | category | flops | bytes accessed | tf_op | source)
XLA Modules:
  0.0 1349.7 jit_solution(5164771268926579444)
XLA Ops:
  7.2 0.0 copy-start
  7.2 0.0 reduce-scatter.3.cloned.1.call-start
  7.2 0.7 reduce-scatter.3.cloned.1.call-update
  7.9 0.0 copy-start.2
  7.9 0.0 all-gather.6.cloned.1.call-start
  8.0 65.1 %reduce-scatter.3.cloned.1.call-done = f32[576,1024]{1,0:T(8,128)} async-done(((f32[1152,1024]{1,0:T(8,128)}), f32[576,1024]{1,0:T(8,128)}) %reduce-scatter.3.cloned.1.call-update) | async-done | bytes 2359312 | tf_op jit(solution)/shard_map/reduce_scatter | solution.py:50
  73.0 0.0 all-gather.6.cloned.1.call-update
  73.1 0.0 all-gather.4.cloned.1.call-start
  73.1 0.7 all-gather.4.cloned.1.call-update
  73.8 0.0 reduce-scatter.5.cloned.1.call-start
  73.8 0.0 copy-done.2
  73.9 0.1 reshape.42
  73.9 0.1 fusion.15
  74.1 0.2 select_reduce_fusion.1
  74.2 0.1 select_reduce_fusion
  74.4 199.3 %all-gather.6.cloned.1.call-done = f32[9216,1024]{1,0:T(8,128)} async-done(((f32[576,1024]{1,0:T(8,128)}), f32[9216,1024]{1,0:T(8,128)}) %all-gather.6.cloned.1.call-update) | async-done | bytes 37748752 | tf_op jit(solution)/shard_map/all_gather | solution.py:51
  273.7 26.5 %gather_fusion = f32[16,576,1024]{2,1,0:T(8,128)} fusion(f32[16,576,1024]{2,1,0:T(8,128)} %bitcast.25, s32[1024]{0:T(1024)S(1)} %pad_clamp_fusion), kind=kCustom, calls=%fused_computation | custom fusion | bytes 75497536 | tf_op jit(solution)/shard_map/jit(_take)/gather | solution.py:52
  300.2 29.8 %broadcast_select_fusion = f32[16,576,1024]{2,1,0:T(8,128)} fusion(f32[16,576,1024]{2,1,0:T(8,128)} %gather_fusion, pred[16]{0:T(512)(128)(4,1)S(1)} %compare_and_fusion), kind=kLoop, calls=%fused_computation.2 | loop fusion | flops 9437184 | bytes 75497488 | tf_op jit(solution)/shard_map/jit(_take)/select_n | solution.py:52
  330.0 443.8 %all_to_all.18 = f32[16,576,1024]{2,1,0:T(8,128)} all-to-all(f32[16,576,1024]{2,1,0:T(8,128)} %broadcast_select_fusion), channel_id=1, replica_groups=mesh['shard'=2,'tensor'=4,'section'=4] {'shard'}, dimensions={0} | all-to-all | bytes 75497472 | tf_op jit(solution)/shard_map/all_to_all | solution.py:53
  773.9 28.0 %copy.29 = f32[8,2,576,1024]{3,2,1,0:T(8,128)} copy(f32[8,2,576,1024]{3,2,0,1:T(8,128)} %bitcast.24) | data formatting | bytes 75497472 | tf_op jit(solution)/shard_map/all_to_all | solution.py:53
  801.8 0.0 copy-done
  801.8 31.9 %fusion.21 = f32[8,1024,72]{1,2,0:T(8,128)} fusion(f32[8,1152,1024]{2,1,0:T(8,128)} %bitcast.21, f32[8,72,1152]{2,1,0:T(8,128)S(1)} %copy-done), kind=kOutput, calls=%fused_computation.36 | convolution fusion | flops 8153726976 | bytes 42762240 | tf_op jit(solution)/shard_map/orf,ofn->orn/dot_general | solution.py:63
  833.8 0.0 all-gather.4.cloned.1.call-done
  833.8 38.4 %multiply_add_fusion = (f32[8,72,1024]{2,1,0:T(8,128)}, f32[8,72,1024]{2,1,0:T(8,128)}) fusion(f32[8,72,1024]{2,1,0:T(8,128)} %param.16, f32[8,72,1024]{2,1,0:T(8,128)} %param.17, f32[8,1024,72]{1,2,0:T(8,128)} %fusion.21, f32[8,1024,1024]{1,2,0:T(8,128)} %all-gather.4.cloned.1.call-done), kind=kOutput, calls=%fused_computation.8 | convolution fusion | flops 7251296256 | bytes 45350912 | tf_op jit(solution)/shard_map/orn,onk->ork/dot_general | solution.py:64
  872.1 27.1 %fusion.5 = f32[8,72,1024]{2,1,0:T(8,128)} fusion(f32[8,1024,1024]{1,2,0:T(8,128)} %all-gather.4.cloned.1.call-done, f32[8,72,1024]{2,1,0:T(8,128)} %get-tuple-element.19, f32[8,72,1024]{2,1,0:T(8,128)} %get-tuple-element.18), kind=kOutput, calls=%fused_computation.12 | convolution fusion | flops 7250116608 | bytes 40632320 | tf_op jit(solution)/shard_map/orn,okn->ork/dot_general | solution.py:70
  899.2 34.9 %convolution_bitcast_fusion = f32[1152,8,1024]{0,2,1:T(8,128)} fusion(f32[8,72,1024]{2,1,0:T(8,128)} %fusion.5, f32[8,72,1152]{2,1,0:T(8,128)S(1)} %copy-done), kind=kOutput, calls=%fused_computation.1 | convolution fusion | flops 8153726976 | bytes 42762240 | tf_op jit(solution)/shard_map/orf,ork->fok/dot_general | solution.py:72
  934.1 37.2 %copy.30 = f32[1152,8,1024]{2,1,0:T(8,128)} copy(f32[1152,8,1024]{0,2,1:T(8,128)} %convolution_bitcast_fusion) | data formatting | bytes 75497472 | tf_op jit(solution)/shard_map/orf,ork->fok/transpose | solution.py:72
  971.3 0.0 reduce-scatter.5.cloned.1.call-update
  971.3 0.0 copy-start.1
  971.3 43.8 %multiply_add_fusion.1 = f32[8,64,1024]{2,1,0:T(8,128)} fusion(f32[8,64,1024]{2,1,0:T(8,128)} %param.13, f32[8,1152,1024]{2,1,0:T(8,128)} %bitcast.22, s32[]{:T(128)S(6)} %select_n.30), kind=kOutput, calls=%fused_computation.18 | convolution fusion | flops 7249330176 | bytes 46661636 | tf_op jit(solution)/shard_map/ofc,ofn->ocn/dot_general | solution.py:60
  1015.2 0.0 copy-done.1
  1015.2 42.9 %fusion.2 = f32[8,72,1152]{2,1,0:T(8,128)} fusion(f32[8,1152,1024]{2,1,0:T(8,128)} %bitcast.23, f32[8,72,1152]{2,1,0:T(8,128)S(1)} %copy-done.1, s32[]{:T(128)S(6)} %select_n.29), kind=kOutput, calls=%fused_computation.6 | convolution fusion | flops 8155717632 | bytes 45416452 | tf_op jit(solution)/shard_map/orn,ofn->orf/dot_general | solution.py:57
  1058.0 280.3 %reduce-scatter.5.cloned.1.call-done = f32[72,8,1024]{2,1,0:T(8,128)} async-done(((f32[1152,8,1024]{2,1,0:T(8,128)}), f32[72,8,1024]{2,1,0:T(8,128)}) %reduce-scatter.5.cloned.1.call-update) | async-done | bytes 2359312 | tf_op jit(solution)/shard_map/reduce_scatter | solution.py:71
  1338.4 4.6 multiply_subtract_fusion
  (5 shorter events, 0.1 us)
Async XLA Ops:
  7.2 794.7 %copy-start = (f32[8,72,1152]{2,1,0:T(8,128)S(1)}, f32[8,72,1152]{2,1,0:T(8,128)}, u32[]{:S(2)}) copy-start(f32[8,72,1152]{2,1,0:T(8,128)} %param.14) | copy-start | bytes 7962628
  7.2 65.9 %reduce-scatter.3.cloned.1.call-start = ((), (), s32[]{:S(2)}) async-start(), calls=%async_computation.3 | async-start | bytes 7077888 | tf_op jit(solution)/shard_map/reduce_scatter | solution.py:50
  7.9 65.9 %copy-start.2 = (s32[4,4]{1,0:T(4,128)S(1)}, s32[4,4]{1,0:T(4,128)}, u32[]{:S(2)}) copy-start(s32[4,4]{1,0:T(4,128)} %param.11) | copy-start | bytes 196
  7.9 265.8 %all-gather.6.cloned.1.call-start = ((), (), s32[]{:S(2)}) async-start(), calls=%async_computation.6 | async-start | bytes 40108032 | tf_op jit(solution)/shard_map/all_gather | solution.py:51
  73.1 760.7 %all-gather.4.cloned.1.call-start = ((), (), s32[]{:S(2)}) async-start(), calls=%async_computation.4 | async-start | bytes 35651584 | tf_op jit(solution)/shard_map/all_gather | solution.py:54
  73.8 1264.6 %reduce-scatter.5.cloned.1.call-start = ((), (), s32[]{:S(2)}) async-start(), calls=%async_computation.5 | async-start | bytes 40108032 | tf_op jit(solution)/shard_map/reduce_scatter | solution.py:71
  971.3 43.8 %copy-start.1 = (f32[8,72,1152]{2,1,0:T(8,128)S(1)}, f32[8,72,1152]{2,1,0:T(8,128)}, u32[]{:S(2)}) copy-start(f32[8,72,1152]{2,1,0:T(8,128)} %param.12) | copy-start | bytes 7962628
Sparse Core Ops, SparseCore 0:
  10.3 62.6 reduce-scatter.2
  74.7 198.9 all-gather.5
  275.3 177.9 all-gather.3
  971.4 366.8 reduce-scatter.4
where the time goes:
time: 1360 us; the launch traced here: 1350 us
  waiting for transfers between devices  546 us (40%)
  blocking collectives  444 us (33%)
  matrix products  219 us (16%)
  local copies, waits for them, and re-layouts  91.8 us (7%)
  other arithmetic  34.8 us (3%)
  between operations  14.1 us (1%)
    all_to_all x1, blocking collectives, local(): lax.all_to_all(ordered, 'shard', split_axis=0, concat_axis=1, tiled=True)  444 us
    reduce_scatter x1, waiting for transfers between devices, local(): lax.psum_scatter(jnp.einsum('orf,ork->fok', left_basis, pulled, precision...  280 us
    all_gather x1, waiting for transfers between devices, local(): lax.all_gather(row_piece[None], ('tensor', 'section'), axis=0, tiled=True)  199 us
    reduce_scatter x1, waiting for transfers between devices, local(): lax.psum_scatter(local_part, 'shard', scatter_dimension=0, tiled=True)  65.1 us
    dot_general x1, matrix products, local(): jnp.einsum('ofc,ofn->ocn', grad_slab, full_grad, precision=exact_mode)  43.8 us
    dot_general x1, matrix products, local(): jnp.einsum('orn,ofn->orf', grad_band, full_grad, precision=exact_mode)  42.9 us
    dot_general x1, matrix products, local(): jnp.einsum('orn,onk->ork', turned, full_right, precision=exact_mode)  38.4 us
    transpose x1, local copies, waits for them, and re-layouts, local(): jnp.einsum('orf,ork->fok', left_basis, pulled, precision=exact_mode)  37.2 us
  transfers between devices with their start and end apart: 4, of which 3 were waited for; matrix products, arithmetic and copies ran while one was open for 15% of the time, Pallas kernels for 0%

commit v1 on v0

--- a/solution.py
+++ b/solution.py
@@ -9,6 +9,12 @@
 learn_rate = 0.01
 decay_weight = 0.1
 step_count = 10
+
+
+def laid_out(blocks, dim):
+    blocks = jnp.moveaxis(blocks, 0, dim)
+    shape = blocks.shape
+    return blocks.reshape(*shape[:dim], shape[dim] * shape[dim + 1], *shape[dim + 2 :])
 
 
 def slot_table(owner_map, shards):
@@ -48,7 +54,23 @@
     col_block = width // members
     local_part = grad_parts[0, 0, 0]
     row_piece = lax.psum_scatter(local_part, "shard", scatter_dimension=0, tiled=True)
-    stacked = lax.all_gather(row_piece[None], ("tensor", "section"), axis=0, tiled=True)
+    size = lax.axis_size(("tensor", "section"))
+    pairs = [(i, (i + 1) % size) for i in range(size)]
+    back = [(b, a) for a, b in pairs]
+    lower, upper = ([], [])
+    for step in range(size - 1):
+        if step % 2 == 0:
+            lower.append(
+                lax.ppermute(lower[-1] if lower else row_piece[None], ("tensor", "section"), pairs)
+            )
+        else:
+            upper.append(
+                lax.ppermute(upper[-1] if upper else row_piece[None], ("tensor", "section"), back)
+            )
+    tiles = jnp.stack([*lower[::-1], row_piece[None], *upper])
+    shift = lax.axis_index(("tensor", "section")) - len(lower)
+    tiles = tiles[(jnp.arange(size) - shift) % size]
+    stacked = laid_out(tiles, 0)
     ordered = jnp.take(stacked, source, axis=0)
     full_grad = lax.all_to_all(ordered, "shard", split_axis=0, concat_axis=1, tiled=True)
     full_right = lax.all_gather(right_basis, ("tensor", "section"), axis=2, tiled=True)

time: 1360 us -> 2070 us (1.52)
  waiting for transfers between devices: 546 us -> 1070 us
  starting transfers between devices: 0.15 us -> 120 us
  local copies, waits for them, and re-layouts: 91.8 us -> 163 us
    ppermute x0 -> x15, waiting for transfers between devices: none -> 719 us  [the longest x8 388 us: local(): lax.ppermute(lower[-1] if lower else row_piece[None], ('tensor', 'section...]
    all_gather x1 -> x0, waiting for transfers between devices: 199 us -> none  [local(): lax.all_gather(row_piece[None], ('tensor', 'section'), axis=0, tiled=True)]
    ppermute x0 -> x15, starting transfers between devices: none -> 119 us  [the longest x8 98.8 us: local(): lax.ppermute(lower[-1] if lower else row_piece[None], ('tensor', 'section...]
    unnamed x6 -> x63, local copies, waits for them, and re-layouts: 0.02 us -> 44.7 us
    gather x0 -> x1, local copies, waits for them, and re-layouts: none -> 25.7 us  [local(): tiles = tiles[(jnp.arange(size) - shift) % size]]
  transfers between devices with their start and end apart: 4 -> 18, of which waited for: 3 -> 16; matrix products, arithmetic and copies ran while one was open for 15% -> 13% of each run, Pallas kernels for 0% -> 0%
where the time goes in v1:
time: 2070 us; the launch traced here: 2060 us
  waiting for transfers between devices  1070 us (52%)
  blocking collectives  439 us (21%)
  matrix products  218 us (11%)
  local copies, waits for them, and re-layouts  163 us (8%)
  starting transfers between devices  120 us (6%)
  other arithmetic  34.3 us (2%)
    all_to_all x1, blocking collectives, local(): lax.all_to_all(ordered, 'shard', split_axis=0, concat_axis=1, tiled=True)  439 us
    ppermute x8, waiting for transfers between devices, local(): lax.ppermute(lower[-1] if lower else row_piece[None], ('tensor', 'section...  388 us
    ppermute x7, waiting for transfers between devices, local(): lax.ppermute(upper[-1] if upper else row_piece[None], ('tensor', 'section...  331 us
    reduce_scatter x1, waiting for transfers between devices, local(): lax.psum_scatter(jnp.einsum('orf,ork->fok', left_basis, pulled, precision...  284 us
    ppermute x8, starting transfers between devices, local(): lax.ppermute(lower[-1] if lower else row_piece[None], ('tensor', 'section...  98.8 us
    reduce_scatter x1, waiting for transfers between devices, local(): lax.psum_scatter(local_part, 'shard', scatter_dimension=0, tiled=True)  64.5 us
    unnamed x63, local copies, waits for them, and re-layouts  44.7 us
    dot_general x1, matrix products, local(): jnp.einsum('ofc,ofn->ocn', grad_slab, full_grad, precision=exact_mode)  43.4 us
  transfers between devices with their start and end apart: 18, of which 16 were waited for; matrix products, arithmetic and copies ran while one was open for 13% of the time, Pallas kernels for 0%

profile of v1, /device:TPU:0, one launch (start us, length us, event | category | flops | bytes accessed | tf_op | source)
XLA Modules:
  0.0 2058.7 jit_solution(16900289826286585545)
XLA Ops:
  9.4 64.5 %reduce-scatter.3.cloned.1.call-done = f32[576,1024]{1,0:T(8,128)} async-done(((f32[1152,1024]{1,0:T(8,128)}), f32[576,1024]{1,0:T(8,128)}) %reduce-scatter.3.cloned.1.call-update) | async-done | bytes 2359312 | tf_op jit(solution)/shard_map/reduce_scatter | solution.py:56
  75.4 80.2 %collective-permute-done = f32[1,576,1024]{2,1,0:T(8,128)S(1)} collective-permute-done((f32[1,576,1024]{2,1,0:T(8,128)}, f32[1,576,1024]{2,1,0:T(8,128)S(1)}, u32[]{:S(2)}, u32[]{:S(2)}) %collective-permute-start) | collective-permute-done | bytes 2359328 | tf_op jit(solution)/shard_map/ppermute | solution.py:64
  157.0 4.4 collective-permute-start.8
  161.4 77.1 %collective-permute-done.1 = f32[1,576,1024]{2,1,0:T(8,128)S(1)} collective-permute-done((f32[1,576,1024]{2,1,0:T(8,128)S(1)}, f32[1,576,1024]{2,1,0:T(8,128)S(1)}, u32[]{:S(2)}, u32[]{:S(2)}) %collective-permute-start.1) | collective-permute-done | bytes 2359328 | tf_op jit(solution)/shard_map/ppermute | solution.py:64
  238.5 57.7 %collective-permute-done.8 = f32[1,576,1024]{2,1,0:T(8,128)S(1)} collective-permute-done((f32[1,576,1024]{2,1,0:T(8,128)}, f32[1,576,1024]{2,1,0:T(8,128)S(1)}, u32[]{:S(2)}, u32[]{:S(2)}) %collective-permute-start.8) | collective-permute-done | bytes 2359328 | tf_op jit(solution)/shard_map/ppermute | solution.py:68
  297.7 5.2 collective-permute-start.9
  302.9 72.5 %collective-permute-done.2 = f32[1,576,1024]{2,1,0:T(8,128)S(1)} collective-permute-done((f32[1,576,1024]{2,1,0:T(8,128)S(1)}, f32[1,576,1024]{2,1,0:T(8,128)S(1)}, u32[]{:S(2)}, u32[]{:S(2)}) %collective-permute-start.2) | collective-permute-done | bytes 2359328 | tf_op jit(solution)/shard_map/ppermute | solution.py:64
  375.4 60.1 %collective-permute-done.9 = f32[1,576,1024]{2,1,0:T(8,128)S(1)} collective-permute-done((f32[1,576,1024]{2,1,0:T(8,128)S(1)}, f32[1,576,1024]{2,1,0:T(8,128)S(1)}, u32[]{:S(2)}, u32[]{:S(2)}) %collective-permute-start.9) | collective-permute-done | bytes 2359328 | tf_op jit(solution)/shard_map/ppermute | solution.py:68
  435.5 4.9 collective-permute-start.10
  440.4 57.0 %collective-permute-done.3 = f32[1,576,1024]{2,1,0:T(8,128)S(1)} collective-permute-done((f32[1,576,1024]{2,1,0:T(8,128)S(1)}, f32[1,576,1024]{2,1,0:T(8,128)S(1)}, u32[]{:S(2)}, u32[]{:S(2)}) %collective-permute-start.3) | collective-permute-done | bytes 2359328 | tf_op jit(solution)/shard_map/ppermute | solution.py:64
  497.5 47.0 %collective-permute-done.10 = f32[1,576,1024]{2,1,0:T(8,128)S(1)} collective-permute-done((f32[1,576,1024]{2,1,0:T(8,128)S(1)}, f32[1,576,1024]{2,1,0:T(8,128)S(1)}, u32[]{:S(2)}, u32[]{:S(2)}) %collective-permute-start.10) | collective-permute-done | bytes 2359328 | tf_op jit(solution)/shard_map/ppermute | solution.py:68
  544.5 3.7 collective-permute-start.11
  548.2 50.2 %collective-permute-done.4 = f32[1,576,1024]{2,1,0:T(8,128)S(1)} collective-permute-done((f32[1,576,1024]{2,1,0:T(8,128)S(1)}, f32[1,576,1024]{2,1,0:T(8,128)S(1)}, u32[]{:S(2)}, u32[]{:S(2)}) %collective-permute-start.4) | collective-permute-done | bytes 2359328 | tf_op jit(solution)/shard_map/ppermute | solution.py:64
  598.4 48.1 %collective-permute-start.5 = (f32[1,576,1024]{2,1,0:T(8,128)S(1)}, f32[1,576,1024]{2,1,0:T(8,128)S(1)}, u32[]{:S(2)}, u32[]{:S(2)}) collective-permute-start(f32[1,576,1024]{2,1,0:T(8,128)S(1)} %collective-permute-done.4), channel_id=1, source_target_pairs={{0,1},{1,2},{2,3},{3,4},{4,5},{5,6},{6,7},{7,8},{8,9},{9,10},{10,1... | collective-permute-start | bytes 7077896 | tf_op jit(solution)/shard_map/ppermute | solution.py:64
  646.5 2.9 collective-permute-done.11
  650.9 2.4 collective-permute-start.12
  653.3 50.0 %collective-permute-done.5 = f32[1,576,1024]{2,1,0:T(8,128)S(1)} collective-permute-done((f32[1,576,1024]{2,1,0:T(8,128)S(1)}, f32[1,576,1024]{2,1,0:T(8,128)S(1)}, u32[]{:S(2)}, u32[]{:S(2)}) %collective-permute-start.5) | collective-permute-done | bytes 2359328 | tf_op jit(solution)/shard_map/ppermute | solution.py:64
  703.3 47.1 %collective-permute-start.6 = (f32[1,576,1024]{2,1,0:T(8,128)S(1)}, f32[1,576,1024]{2,1,0:T(8,128)}, u32[]{:S(2)}, u32[]{:S(2)}) collective-permute-start(f32[1,576,1024]{2,1,0:T(8,128)S(1)} %collective-permute-done.5), channel_id=1, source_target_pairs={{0,1},{1,2},{2,3},{3,4},{4,5},{5,6},{6,7},{7,8},{8,9},{9,10},{10,1... | collective-permute-start | bytes 7077896 | tf_op jit(solution)/shard_map/ppermute | solution.py:64
  750.4 54.0 %collective-permute-done.12 = f32[1,576,1024]{2,1,0:T(8,128)} collective-permute-done((f32[1,576,1024]{2,1,0:T(8,128)S(1)}, f32[1,576,1024]{2,1,0:T(8,128)}, u32[]{:S(2)}, u32[]{:S(2)}) %collective-permute-start.12) | collective-permute-done | bytes 2359328 | tf_op jit(solution)/shard_map/ppermute | solution.py:68
  804.4 2.1 collective-permute-start.7
  807.0 99.1 %collective-permute-done.13 = f32[1,576,1024]{2,1,0:T(8,128)} collective-permute-done((f32[1,576,1024]{2,1,0:T(8,128)}, f32[1,576,1024]{2,1,0:T(8,128)}, u32[]{:S(2)}, u32[]{:S(2)}) %collective-permute-start.13) | collective-permute-done | bytes 2359328 | tf_op jit(solution)/shard_map/ppermute | solution.py:68
  907.0 3.4 bitcast_dynamic-update-slice_fusion.15
  910.4 3.5 bitcast_dynamic-update-slice_fusion.14
  913.9 1.6 bitcast_dynamic-update-slice_fusion.13
  916.5 1.6 bitcast_dynamic-update-slice_fusion.12
  921.5 1.6 bitcast_dynamic-update-slice_fusion.10
  926.5 1.6 bitcast_dynamic-update-slice_fusion.8
  931.6 1.6 bitcast_dynamic-update-slice_fusion.6
  934.1 1.6 bitcast_dynamic-update-slice_fusion.5
  939.1 1.6 bitcast_dynamic-update-slice_fusion.3
  940.7 3.4 bitcast_dynamic-update-slice_fusion.2
  944.1 3.3 bitcast_dynamic-update-slice_fusion.1
  947.4 9.9 collective-permute-done.14
  957.3 1.6 bitcast_dynamic-update-slice_fusion
  958.9 25.7 %gather_fusion = f32[16,576,1024]{2,1,0:T(8,128)} fusion(f32[16,576,1024]{2,1,0:T(8,128)} %bitcast.18, s32[1024]{0:T(1024)S(1)} %pad_clamp_fusion.1), kind=kCustom, calls=%fused_computation | custom fusion | bytes 75497536 | tf_op jit(solution)/shard_map/gather | solution.py:72
  984.7 25.8 %gather_fusion.1 = f32[16,576,1024]{2,1,0:T(8,128)} fusion(f32[16,576,1024]{2,1,0:T(8,128)} %gather_fusion, s32[1024]{0:T(1024)S(1)} %pad_clamp_fusion), kind=kCustom, calls=%fused_computation.1 | custom fusion | bytes 75497536 | tf_op jit(solution)/shard_map/jit(_take)/gather | solution.py:74
  1010.5 29.3 %broadcast_select_fusion = f32[16,576,1024]{2,1,0:T(8,128)} fusion(f32[16,576,1024]{2,1,0:T(8,128)} %gather_fusion.1, pred[16]{0:T(512)(128)(4,1)S(1)} %compare_and_fusion), kind=kLoop, calls=%fused_computation.3 | loop fusion | flops 9437184 | bytes 75497488 | tf_op jit(solution)/shard_map/jit(_take)/select_n | solution.py:74
  1039.8 439.3 %all_to_all.18 = f32[16,576,1024]{2,1,0:T(8,128)} all-to-all(f32[16,576,1024]{2,1,0:T(8,128)} %broadcast_select_fusion), channel_id=1, replica_groups=mesh['shard'=2,'tensor'=4,'section'=4] {'shard'}, dimensions={0} | all-to-all | bytes 75497472 | tf_op jit(solution)/shard_map/all_to_all | solution.py:75
  1479.1 27.9 %copy.24 = f32[2,8,576,1024]{3,2,0,1:T(8,128)} copy(f32[2,8,576,1024]{3,2,1,0:T(8,128)} %bitcast.59) | data formatting | bytes 75497472 | tf_op jit(solution)/shard_map/all_to_all | solution.py:75
  1507.0 31.9 %fusion.23 = f32[8,1024,72]{1,2,0:T(8,128)} fusion(f32[8,1152,1024]{2,1,0:T(8,128)} %bitcast.56, f32[8,72,1152]{2,1,0:T(8,128)S(1)} %copy-done), kind=kOutput, calls=%fused_computation.60 | convolution fusion | flops 8153726976 | bytes 42762240 | tf_op jit(solution)/shard_map/orf,ofn->orn/dot_general | solution.py:85
  1539.0 38.4 %multiply_add_fusion = (f32[8,72,1024]{2,1,0:T(8,128)}, f32[8,72,1024]{2,1,0:T(8,128)}) fusion(f32[8,72,1024]{2,1,0:T(8,128)} %param.16, f32[8,72,1024]{2,1,0:T(8,128)} %param.17, f32[8,1024,72]{1,2,0:T(8,128)} %fusion.23, f32[8,1024,1024]{1,2,0:T(8,128)} %all-gather.2.cloned.1.call-done), kind=kOutput, calls=%fused_computation.9 | convolution fusion | flops 7251296256 | bytes 45350912 | tf_op jit(solution)/shard_map/orn,onk->ork/dot_general | solution.py:86
  1577.3 26.8 %fusion.5 = f32[8,72,1024]{2,1,0:T(8,128)} fusion(f32[8,1024,1024]{1,2,0:T(8,128)} %all-gather.2.cloned.1.call-done, f32[8,72,1024]{2,1,0:T(8,128)} %get-tuple-element.13, f32[8,72,1024]{2,1,0:T(8,128)} %get-tuple-element.12), kind=kOutput, calls=%fused_computation.29 | convolution fusion | flops 7250116608 | bytes 40632320 | tf_op jit(solution)/shard_map/orn,okn->ork/dot_general | solution.py:92
  1604.2 34.8 %convolution_bitcast_fusion = f32[1152,8,1024]{0,2,1:T(8,128)} fusion(f32[8,72,1024]{2,1,0:T(8,128)} %fusion.5, f32[8,72,1152]{2,1,0:T(8,128)S(1)} %copy-done), kind=kOutput, calls=%fused_computation.2 | convolution fusion | flops 8153726976 | bytes 42762240 | tf_op jit(solution)/shard_map/orf,ork->fok/dot_general | solution.py:94
  1639.0 37.3 %copy.25 = f32[1152,8,1024]{2,1,0:T(8,128)} copy(f32[1152,8,1024]{0,2,1:T(8,128)} %convolution_bitcast_fusion) | data formatting | bytes 75497472 | tf_op jit(solution)/shard_map/orf,ork->fok/transpose | solution.py:94
  1676.3 43.4 %multiply_add_fusion.1 = f32[8,64,1024]{2,1,0:T(8,128)} fusion(f32[8,64,1024]{2,1,0:T(8,128)} %param.13, f32[8,1152,1024]{2,1,0:T(8,128)} %bitcast.57, s32[]{:T(128)S(6)} %select_n.56), kind=kOutput, calls=%fused_computation.35 | convolution fusion | flops 7249330176 | bytes 46661636 | tf_op jit(solution)/shard_map/ofc,ofn->ocn/dot_general | solution.py:82
  1719.7 42.8 %fusion.2 = f32[8,72,1152]{2,1,0:T(8,128)} fusion(f32[8,1152,1024]{2,1,0:T(8,128)} %bitcast.58, f32[8,72,1152]{2,1,0:T(8,128)S(1)} %copy-done.1, s32[]{:T(128)S(6)} %select_n.55), kind=kOutput, calls=%fused_computation.7 | convolution fusion | flops 8155717632 | bytes 45416452 | tf_op jit(solution)/shard_map/orn,ofn->orf/dot_general | solution.py:79
  1762.5 284.0 %reduce-scatter.5.cloned.1.call-done = f32[72,8,1024]{2,1,0:T(8,128)} async-done(((f32[1152,8,1024]{2,1,0:T(8,128)}), f32[72,8,1024]{2,1,0:T(8,128)}) %reduce-scatter.5.cloned.1.call-update) | async-done | bytes 2359312 | tf_op jit(solution)/shard_map/reduce_scatter | solution.py:93
  2046.5 4.6 multiply_subtract_fusion
  (79 shorter events, 24.1 us)
Async XLA Ops:
  8.0 1499.0 %copy-start = (f32[8,72,1152]{2,1,0:T(8,128)S(1)}, f32[8,72,1152]{2,1,0:T(8,128)}, u32[]{:S(2)}) copy-start(f32[8,72,1152]{2,1,0:T(8,128)} %param.14) | copy-start | bytes 7962628
  8.0 65.9 %reduce-scatter.3.cloned.1.call-start = ((), (), s32[]{:S(2)}) async-start(), calls=%async_computation.3 | async-start | bytes 7077888 | tf_op jit(solution)/shard_map/reduce_scatter | solution.py:56
  8.1 798.4 %copy-start.23 = (s32[4,4]{1,0:T(4,128)S(1)}, s32[4,4]{1,0:T(4,128)}, u32[]{:S(2)}) copy-start(s32[4,4]{1,0:T(4,128)} %param.11) | copy-start | bytes 196
  8.7 1530.2 %all-gather.2.cloned.1.call-start = ((), (), s32[]{:S(2)}) async-start(), calls=%async_computation.4 | async-start | bytes 35651584 | tf_op jit(solution)/shard_map/all_gather | solution.py:76
  9.3 2037.2 %reduce-scatter.5.cloned.1.call-start = ((), (), s32[]{:S(2)}) async-start(), calls=%async_computation.5 | async-start | bytes 40108032 | tf_op jit(solution)/shard_map/reduce_scatter | solution.py:93
  73.9 81.7 %collective-permute-start = (f32[1,576,1024]{2,1,0:T(8,128)}, f32[1,576,1024]{2,1,0:T(8,128)S(1)}, u32[]{:S(2)}, u32[]{:S(2)}) collective-permute-start(f32[1,576,1024]{2,1,0:T(8,128)} %bitcast.61), channel_id=1, source_target_pairs={{0,1},{1,2},{2,3},{3,4},{4,5},{5,6},{6,7},{7,8},{8,9},{9,10},{10,1... | collective-permute-start | bytes 7077896 | tf_op jit(solution)/shard_map/ppermute | solution.py:64
  155.6 1.4 copy-start.3
  157.0 81.5 %collective-permute-start.1 = (f32[1,576,1024]{2,1,0:T(8,128)S(1)}, f32[1,576,1024]{2,1,0:T(8,128)S(1)}, u32[]{:S(2)}, u32[]{:S(2)}) collective-permute-start(f32[1,576,1024]{2,1,0:T(8,128)S(1)} %collective-permute-done), channel_id=1, source_target_pairs={{0,1},{1,2},{2,3},{3,4},{4,5},{5,6},{6,7},{7,8},{8,9},{9,10},{10,1... | collective-permute-start | bytes 7077896 | tf_op jit(solution)/shard_map/ppermute | solution.py:64
  157.0 139.2 %collective-permute-start.8 = (f32[1,576,1024]{2,1,0:T(8,128)}, f32[1,576,1024]{2,1,0:T(8,128)S(1)}, u32[]{:S(2)}, u32[]{:S(2)}) collective-permute-start(f32[1,576,1024]{2,1,0:T(8,128)} %bitcast.62), channel_id=1, source_target_pairs={{1,0},{2,1},{3,2},{4,3},{5,4},{6,5},{7,6},{8,7},{9,8},{10,9},{11,1... | collective-permute-start | bytes 7077896 | tf_op jit(solution)/shard_map/ppermute | solution.py:68
  238.5 197.1 %copy-start.7 = (f32[1,576,1024]{2,1,0:T(8,128)}, f32[1,576,1024]{2,1,0:T(8,128)S(1)}, u32[]{:S(2)}) copy-start(f32[1,576,1024]{2,1,0:T(8,128)S(1)} %collective-permute-done.1) | copy-start | bytes 7077892
  238.5 137.0 %collective-permute-start.2 = (f32[1,576,1024]{2,1,0:T(8,128)S(1)}, f32[1,576,1024]{2,1,0:T(8,128)S(1)}, u32[]{:S(2)}, u32[]{:S(2)}) collective-permute-start(f32[1,576,1024]{2,1,0:T(8,128)S(1)} %collective-permute-done.1), channel_id=1, source_target_pairs={{0,1},{1,2},{2,3},{3,4},{4,5},{5,6},{6,7},{7,8},{8,9},{9,10},{10,1... | collective-permute-start | bytes 7077896 | tf_op jit(solution)/shard_map/ppermute | solution.py:64
  296.2 1.5 copy-start.5
  297.7 137.8 %collective-permute-start.9 = (f32[1,576,1024]{2,1,0:T(8,128)S(1)}, f32[1,576,1024]{2,1,0:T(8,128)S(1)}, u32[]{:S(2)}, u32[]{:S(2)}) collective-permute-start(f32[1,576,1024]{2,1,0:T(8,128)S(1)} %collective-permute-done.8), channel_id=1, source_target_pairs={{1,0},{2,1},{3,2},{4,3},{5,4},{6,5},{7,6},{8,7},{9,8},{10,9},{11,1... | collective-permute-start | bytes 7077896 | tf_op jit(solution)/shard_map/ppermute | solution.py:68
  375.4 169.0 %copy-start.11 = (f32[1,576,1024]{2,1,0:T(8,128)}, f32[1,576,1024]{2,1,0:T(8,128)S(1)}, u32[]{:S(2)}) copy-start(f32[1,576,1024]{2,1,0:T(8,128)S(1)} %collective-permute-done.2) | copy-start | bytes 7077892
  375.4 122.0 %collective-permute-start.3 = (f32[1,576,1024]{2,1,0:T(8,128)S(1)}, f32[1,576,1024]{2,1,0:T(8,128)S(1)}, u32[]{:S(2)}, u32[]{:S(2)}) collective-permute-start(f32[1,576,1024]{2,1,0:T(8,128)S(1)} %collective-permute-done.2), channel_id=1, source_target_pairs={{0,1},{1,2},{2,3},{3,4},{4,5},{5,6},{6,7},{7,8},{8,9},{9,10},{10,1... | collective-permute-start | bytes 7077896 | tf_op jit(solution)/shard_map/ppermute | solution.py:64
  435.5 4.9 copy-start.9
  435.5 108.9 %collective-permute-start.10 = (f32[1,576,1024]{2,1,0:T(8,128)S(1)}, f32[1,576,1024]{2,1,0:T(8,128)S(1)}, u32[]{:S(2)}, u32[]{:S(2)}) collective-permute-start(f32[1,576,1024]{2,1,0:T(8,128)S(1)} %collective-permute-done.9), channel_id=1, source_target_pairs={{1,0},{2,1},{3,2},{4,3},{5,4},{6,5},{7,6},{8,7},{9,8},{10,9},{11,1... | collective-permute-start | bytes 7077896 | tf_op jit(solution)/shard_map/ppermute | solution.py:68
  497.5 306.9 %copy-start.17 = (f32[1,576,1024]{2,1,0:T(8,128)}, f32[1,576,1024]{2,1,0:T(8,128)S(1)}, u32[]{:S(2)}) copy-start(f32[1,576,1024]{2,1,0:T(8,128)S(1)} %collective-permute-done.3) | copy-start | bytes 7077892
  497.5 101.0 %collective-permute-start.4 = (f32[1,576,1024]{2,1,0:T(8,128)S(1)}, f32[1,576,1024]{2,1,0:T(8,128)S(1)}, u32[]{:S(2)}, u32[]{:S(2)}) collective-permute-start(f32[1,576,1024]{2,1,0:T(8,128)S(1)} %collective-permute-done.3), channel_id=1, source_target_pairs={{0,1},{1,2},{2,3},{3,4},{4,5},{5,6},{6,7},{7,8},{8,9},{9,10},{10,1... | collective-permute-start | bytes 7077896 | tf_op jit(solution)/shard_map/ppermute | solution.py:64
  544.5 3.7 copy-start.13
  544.5 105.0 %collective-permute-start.11 = (f32[1,576,1024]{2,1,0:T(8,128)S(1)}, f32[1,576,1024]{2,1,0:T(8,128)S(1)}, u32[]{:S(2)}, u32[]{:S(2)}) collective-permute-start(f32[1,576,1024]{2,1,0:T(8,128)S(1)} %collective-permute-done.10), channel_id=1, source_target_pairs={{1,0},{2,1},{3,2},{4,3},{5,4},{6,5},{7,6},{8,7},{9,8},{10,9},{11,1... | collective-permute-start | bytes 7077896 | tf_op jit(solution)/shard_map/ppermute | solution.py:68
  598.4 206.0 %copy-start.19 = (f32[1,576,1024]{2,1,0:T(8,128)}, f32[1,576,1024]{2,1,0:T(8,128)S(1)}, u32[]{:S(2)}) copy-start(f32[1,576,1024]{2,1,0:T(8,128)S(1)} %collective-permute-done.4) | copy-start | bytes 7077892
  598.4 104.8 %collective-permute-start.5 = (f32[1,576,1024]{2,1,0:T(8,128)S(1)}, f32[1,576,1024]{2,1,0:T(8,128)S(1)}, u32[]{:S(2)}, u32[]{:S(2)}) collective-permute-start(f32[1,576,1024]{2,1,0:T(8,128)S(1)} %collective-permute-done.4), channel_id=1, source_target_pairs={{0,1},{1,2},{2,3},{3,4},{4,5},{5,6},{6,7},{7,8},{8,9},{9,10},{10,1... | collective-permute-start | bytes 7077896 | tf_op jit(solution)/shard_map/ppermute | solution.py:64
  649.5 1.4 copy-start.15
  650.9 153.5 %collective-permute-start.12 = (f32[1,576,1024]{2,1,0:T(8,128)S(1)}, f32[1,576,1024]{2,1,0:T(8,128)}, u32[]{:S(2)}, u32[]{:S(2)}) collective-permute-start(f32[1,576,1024]{2,1,0:T(8,128)S(1)} %collective-permute-done.11), channel_id=1, source_target_pairs={{1,0},{2,1},{3,2},{4,3},{5,4},{6,5},{7,6},{8,7},{9,8},{10,9},{11,1... | collective-permute-start | bytes 7077896 | tf_op jit(solution)/shard_map/ppermute | solution.py:68
  703.3 101.1 %copy-start.21 = (f32[1,576,1024]{2,1,0:T(8,128)}, f32[1,576,1024]{2,1,0:T(8,128)S(1)}, u32[]{:S(2)}) copy-start(f32[1,576,1024]{2,1,0:T(8,128)S(1)} %collective-permute-done.5) | copy-start | bytes 7077892
  703.3 101.1 %collective-permute-start.6 = (f32[1,576,1024]{2,1,0:T(8,128)S(1)}, f32[1,576,1024]{2,1,0:T(8,128)}, u32[]{:S(2)}, u32[]{:S(2)}) collective-permute-start(f32[1,576,1024]{2,1,0:T(8,128)S(1)} %collective-permute-done.5), channel_id=1, source_target_pairs={{0,1},{1,2},{2,3},{3,4},{4,5},{5,6},{6,7},{7,8},{8,9},{9,10},{10,1... | collective-permute-start | bytes 7077896 | tf_op jit(solution)/shard_map/ppermute | solution.py:64
  804.4 101.7 %collective-permute-start.13 = (f32[1,576,1024]{2,1,0:T(8,128)}, f32[1,576,1024]{2,1,0:T(8,128)}, u32[]{:S(2)}, u32[]{:S(2)}) collective-permute-start(f32[1,576,1024]{2,1,0:T(8,128)} %collective-permute-done.12), channel_id=1, source_target_pairs={{1,0},{2,1},{3,2},{4,3},{5,4},{6,5},{7,6},{8,7},{9,8},{10,9},{11,1... | collective-permute-start | bytes 7077896 | tf_op jit(solution)/shard_map/ppermute | solution.py:68
  804.4 102.6 %collective-permute-start.7 = (f32[1,576,1024]{2,1,0:T(8,128)}, f32[1,576,1024]{2,1,0:T(8,128)}, u32[]{:S(2)}, u32[]{:S(2)}) collective-permute-start(f32[1,576,1024]{2,1,0:T(8,128)} %collective-permute-done.6), channel_id=1, source_target_pairs={{0,1},{1,2},{2,3},{3,4},{4,5},{5,6},{6,7},{7,8},{8,9},{9,10},{10,1... | collective-permute-start | bytes 7077896 | tf_op jit(solution)/shard_map/ppermute | solution.py:64
  906.1 51.2 %collective-permute-start.14 = (f32[1,576,1024]{2,1,0:T(8,128)}, f32[1,576,1024]{2,1,0:T(8,128)S(1)}, u32[]{:S(2)}, u32[]{:S(2)}) collective-permute-start(f32[1,576,1024]{2,1,0:T(8,128)} %collective-permute-done.13), channel_id=1, source_target_pairs={{1,0},{2,1},{3,2},{4,3},{5,4},{6,5},{7,6},{8,7},{9,8},{10,9},{11,1... | collective-permute-start | bytes 7077896 | tf_op jit(solution)/shard_map/ppermute | solution.py:68
  910.4 3.5 copy-start.22
  913.9 2.5 copy-start.20
  916.4 2.5 copy-start.18
  919.0 2.5 copy-start.12
  921.5 2.5 copy-start.8
  924.0 2.5 copy-start.4
  926.5 2.5 copy-start.2
  929.0 2.5 copy-start.6
  931.6 2.5 copy-start.10
  934.1 2.5 copy-start.14
  936.6 2.5 copy-start.16
  1676.3 43.4 %copy-start.1 = (f32[8,72,1152]{2,1,0:T(8,128)S(1)}, f32[8,72,1152]{2,1,0:T(8,128)}, u32[]{:S(2)}) copy-start(f32[8,72,1152]{2,1,0:T(8,128)} %param.12) | copy-start | bytes 7962628
Sparse Core Ops, SparseCore 0:
  11.1 62.7 reduce-scatter.2
Sparse Core Ops, SparseCore 1:
  10.8 498.7 all-gather.1
  1676.4 370.0 reduce-scatter.4
